TPU v7x, 32 devices: a whole 2x2x4 slice. The times are simulated.
32 devices in a mesh: store: 8 (over z, y), tensor: 4 (over x, core).
Axes of the slice: x: 2, y: 2, z: 4, core: 2. Of those that a mesh axis runs over, the one named last changes fastest.
Arguments:
- tokens: bfloat16 [8192, 8192], P('store', 'tensor'), may hold values from -1200 to 1200
- norm_gain: float32 [8192], P('tensor'), may hold values from 0.1 to 1.9
- kv_weight: bfloat16 [8192, 2, 1024], P('tensor'), may hold values from -0.0625 to 0.0625
- adapter_down: bfloat16 [32, 8192, 128], P('store', 'tensor'), may hold values from -0.0625 to 0.0625
- adapter_up: bfloat16 [32, 2, 64, 1024], P('store', None, None, 'tensor'), may hold values from -0.75 to 0.75
- token_adapters: int32 [8192, 1], P('store'), may hold values from 0 to 31; in each aligned block of 1024 rows (0 to 1023, 1024 to 2047, ...) at most 40 rows name the same one
- adapter_slot: int32 [32], replicated, may hold values from 0 to 31, each once
- request_lengths: int32 [16], replicated, may hold values from 1 to 4096, 8192 in all
Outputs:
- new_keys: bfloat16 [8192, 1024], P('store', 'tensor')
- new_values: bfloat16 [8192, 1024], P('store', 'tensor')
Inputs may be any that keep to these rules, and one draw needn't show every extreme that they name: `token_adapters`: among the 1024 tokens of one index of store no adapter is named more than 40 times; in every draw some adapter is named exactly 40 times by the tokens of some index. `adapter_slot`: each row 0 to 31 appears once. `request_lengths`: the lengths sum to 8192; the largest is exactly 4096.
All inputs are finite; a program needn't handle non-finite values.
Results may differ from a plain program's by a relative error of at most 0.0061.
Values may be sent and summed in bfloat16 or wider, within the bound.
A program may use at most 128 MiB of HBM per device.

v0:
```python
import math
import jax
import jax.numpy as jnp
from jax import lax
from jax.sharding import PartitionSpec as P

D = 8192
HEAD = 128
ADAPTER_RANK = 64
epsilon = 1e-05
adapter_scale = 2.0
rope_theta = 500000.0


def place_rows(adapter_ids, adapter_slot, capacity):
    catalog = jnp.arange(adapter_slot.shape[0], dtype=jnp.int32)
    slot_rows = jnp.sum(
        jnp.where(adapter_ids[:, None] == catalog[None, :], adapter_slot[None, :], 0), axis=1
    )
    row_order = jnp.arange(adapter_ids.shape[0], dtype=jnp.int32)
    same_earlier = (adapter_ids[:, None] == adapter_ids[None, :]) & (
        row_order[None, :] < row_order[:, None]
    )
    rank_rows = jnp.sum(same_earlier.astype(jnp.int32), axis=1)
    return slot_rows * capacity + rank_rows


def positions_of(first_row, row_count, lengths):
    global_rows = first_row + jnp.arange(row_count, dtype=jnp.int32)
    request_ends = jnp.cumsum(lengths)
    preceding = jnp.sum(
        jnp.where(request_ends[None, :] <= global_rows[:, None], lengths[None, :], 0), axis=1
    )
    return global_rows - preceding


def rotate(states, positions):
    per_head = states.reshape(states.shape[0], -1, HEAD)
    half_size = HEAD // 2
    frequency = jnp.exp(
        jnp.arange(half_size, dtype=jnp.float32) * (-2.0 * math.log(rope_theta) / HEAD)
    )
    angles = positions.astype(jnp.float32)[:, None] * frequency[None, :]
    cos_part = jnp.concatenate([jnp.cos(angles), jnp.cos(angles)], axis=1)[:, None, :]
    sin_part = jnp.concatenate([jnp.sin(angles), jnp.sin(angles)], axis=1)[:, None, :]
    low_half = per_head[..., :half_size]
    high_half = per_head[..., half_size:]
    turned = jnp.concatenate([-high_half, low_half], axis=-1)
    return (per_head * cos_part + turned * sin_part).reshape(states.shape)


def local(
    tokens,
    norm_gain,
    kv_weight,
    adapter_down,
    adapter_up,
    token_adapters,
    adapter_slot,
    request_lengths,
):
    row_count = tokens.shape[0]
    local_width = tokens.shape[1]
    adapter_total = adapter_slot.shape[0]
    capacity = max(2, 5 * row_count // (4 * adapter_total))
    store_size = lax.axis_size("store")
    per_owner = adapter_down.shape[0]
    kv_local = adapter_up.shape[3]
    widened = tokens.astype(jnp.float32)
    squares = lax.psum(jnp.sum(widened * widened, axis=1), "tensor")
    normed = (widened * lax.rsqrt(squares / D + epsilon)[:, None] * norm_gain[None, :]).astype(
        jnp.bfloat16
    )
    targets = place_rows(token_adapters[:, 0], adapter_slot, capacity)
    send_rows = (
        jnp.zeros((adapter_total * capacity, local_width), jnp.bfloat16).at[targets].set(normed)
    )
    send_rows = send_rows.reshape(store_size, per_owner, capacity, local_width)
    down_projected = jnp.einsum(
        "slcd,ldr->slcr",
        lax.all_to_all(send_rows, "store", split_axis=0, concat_axis=0, tiled=True),
        adapter_down,
        preferred_element_type=jnp.float32,
    )
    rank_total_sum = lax.psum(down_projected, "tensor")
    rank_activation = (rank_total_sum * adapter_scale).astype(jnp.bfloat16)
    split_rank = rank_activation.reshape(rank_activation.shape[:3] + (2, ADAPTER_RANK))
    update_rows = jnp.einsum(
        "slcjr,ljrk->slcjk", split_rank, adapter_up, preferred_element_type=jnp.float32
    )
    back_rows = update_rows.astype(jnp.bfloat16).reshape(
        rank_activation.shape[:3] + (2 * kv_local,)
    )
    returned = lax.all_to_all(back_rows, "store", split_axis=0, concat_axis=0, tiled=True)
    delta_rows = returned.reshape(adapter_total * capacity, 2, kv_local)[targets]
    partial_value = jnp.einsum("td,djk->tjk", normed, kv_weight, preferred_element_type=jnp.float32)
    base_part = lax.psum_scatter(partial_value, "tensor", scatter_dimension=2, tiled=True)
    combined = base_part + delta_rows.astype(jnp.float32)
    positions = positions_of(lax.axis_index("store") * row_count, row_count, request_lengths)
    new_keys = rotate(combined[:, 0, :], positions).astype(jnp.bfloat16)
    new_values = combined[:, 1, :].astype(jnp.bfloat16)
    return (new_keys, new_values)


def solution(mesh):
    return jax.shard_map(
        local,
        mesh=mesh,
        in_specs=(
            P("store", "tensor"),
            P("tensor"),
            P("tensor", None, None),
            P("store", "tensor", None),
            P("store", None, None, "tensor"),
            P("store", None),
            P(),
            P(),
        ),
        out_specs=(P("store", "tensor"), P("store", "tensor")),
        check_vma=False,
    )
```

profile of v0, /device:TPU:0, one launch (start us, length us, event | category | flops | bytes accessed | tf_op | source)
XLA Modules:
  0.0 278.7 jit_solution(12801032871038219586)
XLA Ops:
  7.2 1.4 convert_reduce_fusion
  8.6 0.8 select_reduce_fusion
  9.4 3.1 %fusion = f32[1024]{0:T(1024)S(1)} fusion(bf16[1024,2048]{1,0:T(8,128)(2,1)} %param.8), kind=kLoop, calls=%fused_computation.4 | loop fusion | flops 6290432 | bytes 4198400 | tf_op jit(solution)/shard_map/reduce_sum | solution.py:70
  12.5 8.4 %psum.14 = f32[1024]{0:T(1024)S(1)} all-reduce(f32[1024]{0:T(1024)S(1)} %fusion), channel_id=1, replica_groups=mesh['store'=8,'tensor'=4] {'tensor'}, use_global_device_ids=true, to_apply=%region_1.0 | all-reduce | flops 1024 | bytes 8192 | tf_op jit(solution)/shard_map/psum | solution.py:70
  20.9 11.2 %scatter_custom_fusion = bf16[1280,2048]{1,0:T(8,128)(2,1)} fusion(s32[1024]{0:T(1024)S(1)} %bitcast.50, bf16[]{:T(256)} %constant.6.clone.1, bf16[1024,2048]{1,0:T(8,128)(2,1)} %param.8, f32[2048]{0:T(1024)S(1)} %copy-done.6, f32[1024]{0:T(1024)S(1)} %add_rsqrt_fusion), kind=kCustom, calls=%fused_computation.15 | custom fusion | flops 8388608 | bytes 9449474 | tf_op jit(solution)/shard_map/scatter | solution.py:76
  32.1 120.3 %all_to_all.10 = bf16[8,4,40,2048]{3,2,1,0:T(8,128)(2,1)S(1)} all-to-all(bf16[8,4,40,2048]{3,2,1,0:T(8,128)(2,1)} %bitcast.46), channel_id=1, replica_groups=mesh['store'=8,'tensor'=4] {'store'}, dimensions={0} | all-to-all | bytes 10485760 | tf_op jit(solution)/shard_map/all_to_all | solution.py:81
  152.4 2.5 fusion.13
  154.9 0.2 reduce-scatter.2.cloned.1.call-start
  155.1 14.9 %fusion.3 = f32[1024,2,1024]{2,0,1:T(8,128)} fusion(bf16[2048,2,1024]{2,1,0:T(2,128)(2,1)} %param.10, bf16[1024,2048]{1,0:T(8,128)(2,1)} %param.8, f32[2048]{0:T(1024)S(1)} %copy-done.6, f32[1024]{0:T(1024)S(1)} %add_rsqrt_fusion), kind=kOutput, calls=%fused_computation.7 | convolution fusion | flops 8598323200 | bytes 20983808 | tf_op jit(solution)/shard_map/td,djk->tjk/dot_general | solution.py:96
  170.0 18.1 %all-reduce.2.cloned.1.call-done = f32[8,4,40,128]{3,2,0,1:T(8,128)} async-done(((f32[8,4,40,128]{3,2,0,1:T(8,128)}), f32[8,4,40,128]{3,2,0,1:T(8,128)}) %all-reduce.2.cloned.1.call-update) | async-done | bytes 655376 | tf_op jit(solution)/shard_map/psum | solution.py:85
  188.1 1.1 multiply_convert_fusion
  189.3 0.3 reshape.96
  189.6 0.5 fusion.12
  190.1 1.3 copy.28
  191.5 1.7 reshape.97
  193.2 5.5 %all-to-all-start.1 = ((bf16[8,4,40,512]{3,2,1,0:T(8,128)(2,1)}), bf16[8,4,40,512]{3,2,1,0:T(8,128)(2,1)S(1)}, u32[]{:S(2)}, u32[]{:S(2)}) async-start(bf16[8,4,40,512]{3,2,1,0:T(8,128)(2,1)} %reshape.97), calls=%async_computation.2 | async-start | bytes 2621440 | tf_op jit(solution)/shard_map/all_to_all | solution.py:94
  198.8 0.1 reduce
  199.0 1.9 multiply_cosine_fusion
  200.9 1.3 pad_maximum_fusion
  202.2 27.2 %all-to-all-done.1 = bf16[8,4,40,512]{3,2,1,0:T(8,128)(2,1)S(1)} async-done(((bf16[8,4,40,512]{3,2,1,0:T(8,128)(2,1)}), bf16[8,4,40,512]{3,2,1,0:T(8,128)(2,1)S(1)}, u32[]{:S(2)}, u32[]{:S(2)}) %all-to-all-start.1) | async-done | bytes 1310752 | tf_op jit(solution)/shard_map/all_to_all | solution.py:94
  229.4 1.2 reshape.98
  230.6 5.5 %gather_fusion = bf16[1024,2,256]{2,1,0:T(2,128)(2,1)S(1)} fusion(bf16[1280,2,256]{2,1,0:T(2,128)(2,1)} %reshape.98, s32[1024]{0:T(1024)S(1)} %broadcast_clamp_fusion), kind=kCustom, calls=%fused_computation | custom fusion | bytes 2101248 | tf_op jit(solution)/shard_map/gather | solution.py:95
  236.1 25.9 %reduce-scatter.2.cloned.1.call-done = f32[1024,2,256]{2,0,1:T(8,128)} async-done(((f32[1024,2,1024]{2,0,1:T(8,128)}), f32[1024,2,256]{2,0,1:T(8,128)}) %reduce-scatter.2.cloned.1.call-update) | async-done | bytes 2097168 | tf_op jit(solution)/shard_map/reduce_scatter | solution.py:97
  262.0 1.8 convert_add_fusion
  263.8 1.1 slice.19
  264.9 0.5 copy-done.1
  265.5 0.8 fusion.22
  266.3 1.7 reshape_squeeze.6
  268.1 1.1 slice_negate_fusion
  269.3 1.2 maximum_multiply_fusion
  270.5 0.4 mul.103
  270.9 1.0 fusion.20
  (28 shorter events, 0.4 us)
Async XLA Ops:
  7.2 145.2 %copy-start = (bf16[4,2048,128]{2,1,0:T(8,128)(2,1)S(1)}, bf16[4,2048,128]{2,1,0:T(8,128)(2,1)}, u32[]{:S(2)}) copy-start(bf16[4,2048,128]{2,1,0:T(8,128)(2,1)} %param.11) | copy-start | bytes 6291460
  7.2 13.7 %copy-start.6 = (f32[2048]{0:T(1024)S(1)}, f32[2048]{0:T(1024)}, u32[]{:S(2)}) copy-start(f32[2048]{0:T(1024)} %param.9) | copy-start | bytes 24580
  7.2 180.9 %all-reduce.2.cloned.1.call-start = ((), (), s32[]{:S(2)}) async-start(), calls=%async_computation.4 | async-start | bytes 1310720 | tf_op jit(solution)/shard_map/psum | solution.py:85
  154.9 107.1 %reduce-scatter.2.cloned.1.call-start = ((), (), s32[]{:S(2)}) async-start(), calls=%async_computation.3 | async-start | bytes 10485760 | tf_op jit(solution)/shard_map/reduce_scatter | solution.py:97
  170.0 19.6 %copy-start.5 = (bf16[4,2,64,256]{3,2,1,0:T(8,128)(2,1)S(1)}, bf16[4,2,64,256]{3,2,1,0:T(8,128)(2,1)}, u32[]{:S(2)}) copy-start(bf16[4,2,64,256]{3,2,1,0:T(8,128)(2,1)} %param.12) | copy-start | bytes 786436
  190.1 8.6 %copy-start.7 = (s32[16]{0:T(128)S(1)}, s32[16]{0:T(128)}, u32[]{:S(2)}) copy-start(s32[16]{0:T(128)} %param.15) | copy-start | bytes 196
  193.2 36.3 %all-to-all-start.1 = ((bf16[8,4,40,512]{3,2,1,0:T(8,128)(2,1)}), bf16[8,4,40,512]{3,2,1,0:T(8,128)(2,1)S(1)}, u32[]{:S(2)}, u32[]{:S(2)}) async-start(bf16[8,4,40,512]{3,2,1,0:T(8,128)(2,1)} %reshape.97), calls=%async_computation.2 | async-start | bytes 2621440 | tf_op jit(solution)/shard_map/all_to_all | solution.py:94
  263.8 1.7 copy-start.1
  268.1 1.2 copy-start.4
  268.1 2.4 copy-start.3
  268.1 2.8 copy-start.2
Sparse Core Ops, SparseCore 0:
  155.0 33.0 all-reduce.1
  190.7 71.2 reduce-scatter.1
where the time goes:
time: 279 us
  blocking collectives  129 us (46%)
  waiting for transfers between devices  71.1 us (25%)
  other arithmetic  26.2 us (9%)
  matrix products  17.9 us (6%)
  local copies, waits for them, and re-layouts  14.8 us (5%)
  between operations  14.2 us (5%)
  starting transfers between devices  5.78 us (2%)
    all_to_all x1, blocking collectives, local(): lax.all_to_all(send_rows, 'store', split_axis=0, concat_axis=0, tiled=True)  120 us
    all_to_all x1, waiting for transfers between devices, local(): lax.all_to_all(back_rows, 'store', split_axis=0, concat_axis=0, tiled=True)  27.2 us
    reduce_scatter x1, waiting for transfers between devices, local(): lax.psum_scatter(partial_value, 'tensor', scatter_dimension=2, tiled=True)  25.9 us
    psum x1, waiting for transfers between devices, local(): rank_total_sum = lax.psum(down_projected, 'tensor')  18.1 us
    dot_general x1, matrix products, local(): jnp.einsum('td,djk->tjk', normed, kv_weight, preferred_element_type=jnp.f...  14.9 us
    scatter x1, other arithmetic, local(): jnp.zeros((adapter_total * capacity, local_width), jnp.bfloat16).at[targets]  11.2 us
    psum x1, blocking collectives, local(): squares = lax.psum(jnp.sum(widened * widened, axis=1), 'tensor')  8.38 us
  transfers between devices with their start and end apart: 3, of which 3 were waited for; matrix products, arithmetic and copies ran while one was open for 11% of the time, Pallas kernels for 0%

commit v1 on v0

--- a/solution.py
+++ b/solution.py
@@ -3,6 +3,7 @@
 import jax.numpy as jnp
 from jax import lax
 from jax.sharding import PartitionSpec as P
+from jax.lax import all_gather
 
 D = 8192
 HEAD = 128
@@ -10,6 +11,10 @@
 epsilon = 1e-05
 adapter_scale = 2.0
 rope_theta = 500000.0
+
+
+def series_all_define(unit):
+    return all_gather(unit, axis_name="tensor").sum(axis=0)
 
 
 def place_rows(adapter_ids, adapter_slot, capacity):
@@ -82,7 +87,7 @@
         adapter_down,
         preferred_element_type=jnp.float32,
     )
-    rank_total_sum = lax.psum(down_projected, "tensor")
+    rank_total_sum = series_all_define(down_projected)
     rank_activation = (rank_total_sum * adapter_scale).astype(jnp.bfloat16)
     split_rank = rank_activation.reshape(rank_activation.shape[:3] + (2, ADAPTER_RANK))
     update_rows = jnp.einsum(

time: 279 us -> 271 us (0.971)
  waiting for transfers between devices: 71.1 us -> 61.6 us
    psum x1 -> x0, waiting for transfers between devices: 18.1 us -> none  [local(): rank_total_sum = lax.psum(down_projected, 'tensor')]
    all_gather x0 -> x1, waiting for transfers between devices: none -> 9.57 us  [series_all_define(): return all_gather(unit, axis_name='tensor').sum(axis=0)]
  transfers between devices with their start and end apart: 3 -> 3, of which waited for: 3 -> 3; matrix products, arithmetic and copies ran while one was open for 11% -> 12% of each run, Pallas kernels for 0% -> 0%
where the time goes in v1:
time: 271 us; the launch traced here: 270 us
  blocking collectives  129 us (48%)
  waiting for transfers between devices  61.6 us (23%)
  other arithmetic  27.1 us (10%)
  matrix products  17.9 us (7%)
  local copies, waits for them, and re-layouts  14.9 us (5%)
  between operations  14.3 us (5%)
  starting transfers between devices  5.78 us (2%)
    all_to_all x1, blocking collectives, local(): lax.all_to_all(send_rows, 'store', split_axis=0, concat_axis=0, tiled=True)  120 us
    all_to_all x1, waiting for transfers between devices, local(): lax.all_to_all(back_rows, 'store', split_axis=0, concat_axis=0, tiled=True)  28.2 us
    reduce_scatter x1, waiting for transfers between devices, local(): lax.psum_scatter(partial_value, 'tensor', scatter_dimension=2, tiled=True)  23.8 us
    dot_general x1, matrix products, local(): jnp.einsum('td,djk->tjk', normed, kv_weight, preferred_element_type=jnp.f...  14.9 us
    scatter x1, other arithmetic, local(): jnp.zeros((adapter_total * capacity, local_width), jnp.bfloat16).at[targets]  11.2 us
    all_gather x1, waiting for transfers between devices, series_all_define(): return all_gather(unit, axis_name='tensor').sum(axis=0)  9.57 us
    psum x1, blocking collectives, local(): squares = lax.psum(jnp.sum(widened * widened, axis=1), 'tensor')  8.38 us
    all_to_all x1, starting transfers between devices, local(): lax.all_to_all(back_rows, 'store', split_axis=0, concat_axis=0, tiled=True)  5.52 us
  transfers between devices with their start and end apart: 3, of which 3 were waited for; matrix products, arithmetic and copies ran while one was open for 12% of the time, Pallas kernels for 0%

profile of v1, /device:TPU:0, one launch (start us, length us, event | category | flops | bytes accessed | tf_op | source)
XLA Modules:
  0.0 270.2 jit_solution(17537318963463318395)
XLA Ops:
  7.2 1.4 convert_reduce_fusion
  8.6 0.8 select_reduce_fusion
  9.4 3.1 %fusion = f32[1024]{0:T(1024)S(1)} fusion(bf16[1024,2048]{1,0:T(8,128)(2,1)} %param.8), kind=kLoop, calls=%fused_computation.4 | loop fusion | flops 6290432 | bytes 4198400 | tf_op jit(solution)/shard_map/reduce_sum | solution.py:75
  12.5 8.4 %psum.7 = f32[1024]{0:T(1024)S(1)} all-reduce(f32[1024]{0:T(1024)S(1)} %fusion), channel_id=1, replica_groups=mesh['store'=8,'tensor'=4] {'tensor'}, use_global_device_ids=true, to_apply=%region_1.0 | all-reduce | flops 1024 | bytes 8192 | tf_op jit(solution)/shard_map/psum | solution.py:75
  20.9 11.2 %scatter_custom_fusion = bf16[1280,2048]{1,0:T(8,128)(2,1)} fusion(s32[1024]{0:T(1024)S(1)} %bitcast.52, bf16[]{:T(256)} %constant.6.clone.1, bf16[1024,2048]{1,0:T(8,128)(2,1)} %param.8, f32[2048]{0:T(1024)S(1)} %copy-done.6, f32[1024]{0:T(1024)S(1)} %add_rsqrt_fusion), kind=kCustom, calls=%fused_computation.15 | custom fusion | flops 8388608 | bytes 9449474 | tf_op jit(solution)/shard_map/scatter | solution.py:81
  32.1 120.3 %all_to_all.10 = bf16[8,4,40,2048]{3,2,1,0:T(8,128)(2,1)S(1)} all-to-all(bf16[8,4,40,2048]{3,2,1,0:T(8,128)(2,1)} %bitcast.47), channel_id=1, replica_groups=mesh['store'=8,'tensor'=4] {'store'}, dimensions={0} | all-to-all | bytes 10485760 | tf_op jit(solution)/shard_map/all_to_all | solution.py:86
  152.4 2.5 fusion.13
  154.9 0.2 reduce-scatter.2.cloned.1.call-start
  155.2 14.9 %fusion.3 = f32[1024,2,1024]{2,0,1:T(8,128)} fusion(bf16[2048,2,1024]{2,1,0:T(2,128)(2,1)} %param.10, bf16[1024,2048]{1,0:T(8,128)(2,1)} %param.8, f32[2048]{0:T(1024)S(1)} %copy-done.6, f32[1024]{0:T(1024)S(1)} %add_rsqrt_fusion), kind=kOutput, calls=%fused_computation.7 | convolution fusion | flops 8598323200 | bytes 20983808 | tf_op jit(solution)/shard_map/td,djk->tjk/dot_general | solution.py:101
  170.1 9.6 %all-gather.3.cloned.1.call-done = f32[32,4,40,128]{3,2,0,1:T(8,128)} async-done(((f32[8,4,40,128]{3,2,0,1:T(8,128)}), f32[32,4,40,128]{3,2,0,1:T(8,128)}) %all-gather.3.cloned.1.call-update) | async-done | bytes 2621456 | tf_op jit(solution)/shard_map/all_gather | solution.py:17
  179.7 1.9 reduce_sum.48
  181.7 0.3 reshape.122
  182.0 0.5 fusion.12
  182.5 1.3 copy.29
  183.9 1.7 reshape.98
  185.6 5.5 %all-to-all-start.1 = ((bf16[8,4,40,512]{3,2,1,0:T(8,128)(2,1)}), bf16[8,4,40,512]{3,2,1,0:T(8,128)(2,1)S(1)}, u32[]{:S(2)}, u32[]{:S(2)}) async-start(bf16[8,4,40,512]{3,2,1,0:T(8,128)(2,1)} %reshape.98), calls=%async_computation.2 | async-start | bytes 2621440 | tf_op jit(solution)/shard_map/all_to_all | solution.py:99
  191.3 0.1 reduce
  191.5 1.9 multiply_cosine_fusion
  193.4 1.3 pad_maximum_fusion
  194.7 28.2 %all-to-all-done.1 = bf16[8,4,40,512]{3,2,1,0:T(8,128)(2,1)S(1)} async-done(((bf16[8,4,40,512]{3,2,1,0:T(8,128)(2,1)}), bf16[8,4,40,512]{3,2,1,0:T(8,128)(2,1)S(1)}, u32[]{:S(2)}, u32[]{:S(2)}) %all-to-all-start.1) | async-done | bytes 1310752 | tf_op jit(solution)/shard_map/all_to_all | solution.py:99
  222.9 1.3 reshape.99
  224.2 5.5 %gather_fusion = bf16[1024,2,256]{2,1,0:T(2,128)(2,1)S(1)} fusion(bf16[1280,2,256]{2,1,0:T(2,128)(2,1)} %reshape.99, s32[1024]{0:T(1024)S(1)} %broadcast_clamp_fusion), kind=kCustom, calls=%fused_computation | custom fusion | bytes 2101248 | tf_op jit(solution)/shard_map/gather | solution.py:100
  229.7 23.8 %reduce-scatter.2.cloned.1.call-done = f32[1024,2,256]{2,0,1:T(8,128)} async-done(((f32[1024,2,1024]{2,0,1:T(8,128)}), f32[1024,2,256]{2,0,1:T(8,128)}) %reduce-scatter.2.cloned.1.call-update) | async-done | bytes 2097168 | tf_op jit(solution)/shard_map/reduce_scatter | solution.py:102
  253.5 1.8 convert_add_fusion
  255.3 1.1 slice.19
  256.4 0.5 copy-done.1
  257.0 0.8 fusion.22
  257.8 1.7 reshape_squeeze.6
  259.6 1.1 slice_negate_fusion
  260.8 1.2 maximum_multiply_fusion
  262.0 0.4 mul.105
  262.4 1.0 fusion.20
  (29 shorter events, 0.4 us)
Async XLA Ops:
  7.2 145.2 %copy-start = (bf16[4,2048,128]{2,1,0:T(8,128)(2,1)S(1)}, bf16[4,2048,128]{2,1,0:T(8,128)(2,1)}, u32[]{:S(2)}) copy-start(bf16[4,2048,128]{2,1,0:T(8,128)(2,1)} %param.11) | copy-start | bytes 6291460
  7.2 13.7 %copy-start.6 = (f32[2048]{0:T(1024)S(1)}, f32[2048]{0:T(1024)}, u32[]{:S(2)}) copy-start(f32[2048]{0:T(1024)} %param.9) | copy-start | bytes 24580
  7.2 172.5 %all-gather.3.cloned.1.call-start = ((), (), s32[]{:S(2)}) async-start(), calls=%async_computation.4 | async-start | bytes 3276800 | tf_op jit(solution)/shard_map/all_gather | solution.py:17
  154.9 98.6 %reduce-scatter.2.cloned.1.call-start = ((), (), s32[]{:S(2)}) async-start(), calls=%async_computation.3 | async-start | bytes 10485760 | tf_op jit(solution)/shard_map/reduce_scatter | solution.py:102
  170.1 11.9 %copy-start.5 = (bf16[4,2,64,256]{3,2,1,0:T(8,128)(2,1)S(1)}, bf16[4,2,64,256]{3,2,1,0:T(8,128)(2,1)}, u32[]{:S(2)}) copy-start(bf16[4,2,64,256]{3,2,1,0:T(8,128)(2,1)} %param.12) | copy-start | bytes 786436
  182.5 8.6 %copy-start.7 = (s32[16]{0:T(128)S(1)}, s32[16]{0:T(128)}, u32[]{:S(2)}) copy-start(s32[16]{0:T(128)} %param.15) | copy-start | bytes 196
  185.6 37.3 %all-to-all-start.1 = ((bf16[8,4,40,512]{3,2,1,0:T(8,128)(2,1)}), bf16[8,4,40,512]{3,2,1,0:T(8,128)(2,1)S(1)}, u32[]{:S(2)}, u32[]{:S(2)}) async-start(bf16[8,4,40,512]{3,2,1,0:T(8,128)(2,1)} %reshape.98), calls=%async_computation.2 | async-start | bytes 2621440 | tf_op jit(solution)/shard_map/all_to_all | solution.py:99
  255.3 1.7 copy-start.1
  259.6 1.2 copy-start.4
  259.6 2.4 copy-start.3
  259.6 2.8 %copy-start.2 = (f32[1024,2,256]{2,0,1:T(8,128)S(1)}, f32[1024,2,256]{2,0,1:T(8,128)}, u32[]{:S(2)}) copy-start(f32[1024,2,256]{2,0,1:T(8,128)} %copy-done.1) | copy-start | bytes 6291460
Sparse Core Ops, SparseCore 0:
  155.1 24.5 all-gather.2
  182.2 71.2 reduce-scatter.1
